TPU v7x, 32 devices: a whole 2x2x4 slice. The times are simulated.
32 devices in a mesh: depth: 4 (over y, x), xline: 8 (over z, core).
Axes of the slice: x: 2, y: 2, z: 4, core: 2. Of those that a mesh axis runs over, the one named last changes fastest.
Arguments:
- receiver_data: bfloat16 [4, 2, 1024, 1024], P(None, None, None, 'xline'), may hold values from -6 to 6
- source_amp: bfloat16 [4, 2, 256], replicated, may hold values from -6 to 6
- source_x: int32 [256], replicated, may hold values from 0 to 1023
- source_y: int32 [256], replicated, may hold values from 0 to 1023
- omegas: float32 [4], replicated, may hold values from 0.5 to 3
- slowness: float32 [4, 1024, 1024], P('depth', None, 'xline'), may hold values from 0.2 to 2
- inverses: bfloat16 [4, 4, 2, 256, 256], replicated, may hold values from -0.1875 to 0.1875
- zones_x: int32 [4, 4], P('depth'), may hold values from 0 to 3
- zones_y: int32 [4, 4], P('depth'), may hold values from 0 to 3
Outputs:
- gradient: float32 [4, 1024, 1024], P('depth', None, 'xline')
All inputs are finite; a program needn't handle non-finite values.
Results may differ from a plain program's by a relative error of at most 0.015.
Values may be sent and summed in bfloat16 or wider, within the bound.
A program may use at most 64 MiB of HBM per device.

v0:
```python
import jax
import jax.numpy as jnp
from jax import lax
from jax.sharding import PartitionSpec as P


def partner(block, axis, bit):
    count = lax.axis_size(axis)
    route = []
    for low in range(count):
        high = low | 1 << bit
        if high != low and high < count:
            route += [(low, high), (high, low)]
    return lax.ppermute(block, axis, route)


def from_behind(value, axis, by):
    size = lax.axis_size(axis)
    pairs = [(i, i + by) for i in range(size) if 0 <= i + by < size]
    return lax.ppermute(value, axis, pairs)


def rotate(field, angle, sign):
    field_real = field[0].astype(jnp.float32)
    field_imag = field[1].astype(jnp.float32)
    cosine = jnp.cos(angle)
    sine = jnp.sin(angle) * sign
    return jnp.stack(
        [field_real * cosine - field_imag * sine, field_real * sine + field_imag * cosine]
    ).astype(jnp.bfloat16)


def complex_apply(parts, k_real, k_imag, form):

    def blockwise(matrix, vector):
        return jnp.einsum(form, matrix, vector, preferred_element_type=jnp.float32)

    out_real = (
        parts[0].astype(jnp.float32) + blockwise(k_real, parts[0]) - blockwise(k_imag, parts[1])
    )
    out_imag = (
        parts[1].astype(jnp.float32) + blockwise(k_real, parts[1]) + blockwise(k_imag, parts[0])
    )
    return jnp.stack([out_real, out_imag]).astype(jnp.bfloat16)


def solve_inline(field, blocks, sign):
    order = blocks.shape[2]
    parts = field.reshape(2, field.shape[1] // order, order, field.shape[2])
    k_imag = blocks[:, 1] if sign > 0 else -blocks[:, 1]
    return complex_apply(parts, blocks[:, 0], k_imag, "bij,bjy->biy").reshape(field.shape)


def solve_crossline(field, blocks, sign):
    order = blocks.shape[2]
    parts = field.reshape(2, field.shape[1], field.shape[2] // order, order)
    k_imag = blocks[:, 1] if sign > 0 else -blocks[:, 1]
    return complex_apply(parts, blocks[:, 0], k_imag, "bij,xbj->xbi").reshape(field.shape)


def per_device(
    receiver_data, source_amp, source_x, source_y, omegas, slowness, inverses, zones_x, zones_y
):
    sections = lax.axis_size("depth")
    line_index = lax.axis_index("xline")
    section = lax.axis_index("depth")
    freqs, _, width_x, width_y = receiver_data.shape
    levels = slowness.shape[0]
    onehot_x = (jnp.arange(width_x)[:, None] == source_x[None, :]).astype(jnp.bfloat16)
    local_y = source_y - line_index * width_y
    onehot_y = (local_y[:, None] == jnp.arange(width_y)[None, :]).astype(jnp.bfloat16)
    spread = source_amp[:, :, :, None] * onehot_y[None, None]
    sources = jnp.einsum(
        "xs,fcsy->fcxy", onehot_x, spread, preferred_element_type=jnp.float32
    ).astype(jnp.bfloat16)
    half = width_x // 2
    parity = line_index % 2

    def crossline_step(src_field, rec_field, table, zone_row):
        mine_start = parity * half
        other_start = (1 - parity) * half
        outgoing = (
            lax.dynamic_slice_in_dim(src_field, other_start, half, 1),
            lax.dynamic_slice_in_dim(rec_field, other_start, half, 1),
        )
        incoming = partner((outgoing[0], outgoing[1]), "xline", 0)

        def assemble(kept, got, axis):
            return jnp.where(
                parity == 0, jnp.concatenate([kept, got], axis), jnp.concatenate([got, kept], axis)
            )

        block_src = assemble(
            lax.dynamic_slice_in_dim(src_field, mine_start, half, 1), incoming[0], 2
        )
        block_rec = assemble(
            lax.dynamic_slice_in_dim(rec_field, mine_start, half, 1), incoming[1], 2
        )
        blocks = jnp.take(table, lax.dynamic_slice_in_dim(zone_row, line_index // 2, 1), axis=0)
        solved_src = solve_crossline(block_src, blocks, 1.0)
        solved_rec = solve_crossline(block_rec, blocks, -1.0)
        other_rows = (1 - parity) * width_y
        mine_rows = parity * width_y
        returned = partner(
            (
                lax.dynamic_slice_in_dim(solved_src, other_rows, width_y, 2),
                lax.dynamic_slice_in_dim(solved_rec, other_rows, width_y, 2),
            ),
            "xline",
            0,
        )
        new_src = assemble(
            lax.dynamic_slice_in_dim(solved_src, mine_rows, width_y, 2), returned[0], 1
        )
        new_rec = assemble(
            lax.dynamic_slice_in_dim(solved_rec, mine_rows, width_y, 2), returned[1], 1
        )
        return (new_src, new_rec)

    def level_update(src_field, rec_field, table, omega, slow_level, zone_row_x, zone_row_y):
        angle = omega * slow_level
        inline_blocks = jnp.take(table, zone_row_x, axis=0)
        src_field = solve_inline(rotate(src_field, angle, 1.0), inline_blocks, 1.0)
        rec_field = solve_inline(rotate(rec_field, angle, -1.0), inline_blocks, -1.0)
        src_field, rec_field = crossline_step(src_field, rec_field, table, zone_row_y)
        correlation = src_field[0].astype(jnp.float32) * rec_field[0].astype(
            jnp.float32
        ) + src_field[1].astype(jnp.float32) * rec_field[1].astype(jnp.float32)
        return (src_field, rec_field, correlation)

    def segment(step, carry):
        src_field, rec_field, gradient = carry
        passed_src, passed_rec = from_behind((src_field, rec_field), "depth", 1)
        freq = step - section
        valid = (freq >= 0) & (freq < freqs)
        freq_index = jnp.clip(freq, 0, freqs - 1)
        first = section == 0
        src_field = jnp.where(
            first, lax.dynamic_index_in_dim(sources, freq_index, 0, keepdims=False), passed_src
        )
        rec_field = jnp.where(
            first,
            lax.dynamic_index_in_dim(receiver_data, freq_index, 0, keepdims=False),
            passed_rec,
        )
        table = lax.dynamic_index_in_dim(inverses, freq_index, 0, keepdims=False)
        omega = lax.dynamic_index_in_dim(omegas, freq_index, 0, keepdims=False)
        weight = jnp.where(valid, omega * omega, 0.0)
        src_field, rec_field, correlation = level_update(
            src_field, rec_field, table, omega, slowness[0], zones_x[0], zones_y[0]
        )
        gradient = gradient.at[0].add(weight * correlation)
        return (src_field, rec_field, gradient)

    empty_field = jnp.zeros((2, width_x, width_y), jnp.bfloat16)
    start = (empty_field, empty_field, jnp.zeros((levels, width_x, width_y), jnp.float32))
    final = lax.fori_loop(0, freqs + sections - 1, segment, start)
    return final[2]


def solution(mesh):
    in_specs = (
        P(None, None, None, "xline"),
        P(),
        P(),
        P(),
        P(),
        P("depth", None, "xline"),
        P(),
        P("depth", None),
        P("depth", None),
    )
    out_specs = P("depth", None, "xline")
    return jax.shard_map(
        per_device, mesh=mesh, in_specs=in_specs, out_specs=out_specs, check_vma=False
    )
```

profile of v0, /device:TPU:6, one launch (start us, length us, event | category | flops | bytes accessed | tf_op | source)
XLA Modules:
  0.0 310.1 jit_solution(13906270498325018447)
XLA Ops:
  3.9 2.8 convert_bitcast_fusion
  6.7 303.4 %while.24 = (s32[]{:T(128)}, bf16[2,1024,128]{2,1,0:T(8,128)(2,1)S(1)}, bf16[2,1024,128]{2,1,0:T(8,128)(2,1)S(1)}, f32[1,1024,128]{2,1,0:T(8,128)}, pred[]{:T(51...) while((s32[]{:T(128)}, ...), condition=%wide.wide.region_1.2_spmd.clone, body=%wide.wide.region_0.1_spmd.clone.sunk | while | flops 1098122240 | bytes 59773684 | solution.py:157
  16.1 8.4 %collective-permute-done.1 = bf16[2,1024,128]{2,1,0:T(8,128)(2,1)S(1)} collective-permute-done((bf16[2,1024,128]{2,1,0:T(8,128)(2,1)}, bf16[2,1024,128]{2,1,0:T(8,128)(2,1)S(1)}, u32[]{:S(2)}, u32[]{:S(2)}) %collective-permute-start.1) | collective-permute-done | bytes 524320 | tf_op jit(solution)/shard_map/while/body/eval_jaxpr/ppermute | solution.py:20
  24.6 10.2 %collective-permute-done = bf16[2,1024,128]{2,1,0:T(8,128)(2,1)} collective-permute-done((bf16[2,1024,128]{2,1,0:T(8,128)(2,1)}, bf16[2,1024,128]{2,1,0:T(8,128)(2,1)}, u32[]{:S(2)}, u32[]{:S(2)}) %collective-permute-start) | collective-permute-done | bytes 524320 | tf_op jit(solution)/shard_map/while/body/eval_jaxpr/ppermute | solution.py:20
  36.0 2.8 fusion.102
  57.6 8.4 %collective-permute-done.1 = bf16[2,1024,128]{2,1,0:T(8,128)(2,1)S(1)} collective-permute-done((bf16[2,1024,128]{2,1,0:T(8,128)(2,1)}, bf16[2,1024,128]{2,1,0:T(8,128)(2,1)S(1)}, u32[]{:S(2)}, u32[]{:S(2)}) %collective-permute-start.1) | collective-permute-done | bytes 524320 | tf_op jit(solution)/shard_map/while/body/eval_jaxpr/ppermute | solution.py:20
  66.0 10.6 %collective-permute-done = bf16[2,1024,128]{2,1,0:T(8,128)(2,1)} collective-permute-done((bf16[2,1024,128]{2,1,0:T(8,128)(2,1)}, bf16[2,1024,128]{2,1,0:T(8,128)(2,1)}, u32[]{:S(2)}, u32[]{:S(2)}) %collective-permute-start) | collective-permute-done | bytes 524320 | tf_op jit(solution)/shard_map/while/body/eval_jaxpr/ppermute | solution.py:20
  77.9 2.8 fusion.102
  89.2 2.0 multiply_add_fusion.2
  100.5 8.7 %collective-permute-done.1 = bf16[2,1024,128]{2,1,0:T(8,128)(2,1)S(1)} collective-permute-done((bf16[2,1024,128]{2,1,0:T(8,128)(2,1)}, bf16[2,1024,128]{2,1,0:T(8,128)(2,1)S(1)}, u32[]{:S(2)}, u32[]{:S(2)}) %collective-permute-start.1) | collective-permute-done | bytes 524320 | tf_op jit(solution)/shard_map/while/body/eval_jaxpr/ppermute | solution.py:20
  109.3 10.9 %collective-permute-done = bf16[2,1024,128]{2,1,0:T(8,128)(2,1)} collective-permute-done((bf16[2,1024,128]{2,1,0:T(8,128)(2,1)}, bf16[2,1024,128]{2,1,0:T(8,128)(2,1)}, u32[]{:S(2)}, u32[]{:S(2)}) %collective-permute-start) | collective-permute-done | bytes 524320 | tf_op jit(solution)/shard_map/while/body/eval_jaxpr/ppermute | solution.py:20
  121.4 2.8 fusion.102
  132.7 2.0 multiply_add_fusion.2
  140.1 1.3 dynamic-slice_bitcast_fusion.2
  144.1 9.0 %collective-permute-done.1 = bf16[2,1024,128]{2,1,0:T(8,128)(2,1)S(1)} collective-permute-done((bf16[2,1024,128]{2,1,0:T(8,128)(2,1)}, bf16[2,1024,128]{2,1,0:T(8,128)(2,1)S(1)}, u32[]{:S(2)}, u32[]{:S(2)}) %collective-permute-start.1) | collective-permute-done | bytes 524320 | tf_op jit(solution)/shard_map/while/body/eval_jaxpr/ppermute | solution.py:20
  153.1 10.9 %collective-permute-done = bf16[2,1024,128]{2,1,0:T(8,128)(2,1)} collective-permute-done((bf16[2,1024,128]{2,1,0:T(8,128)(2,1)}, bf16[2,1024,128]{2,1,0:T(8,128)(2,1)}, u32[]{:S(2)}, u32[]{:S(2)}) %collective-permute-start) | collective-permute-done | bytes 524320 | tf_op jit(solution)/shard_map/while/body/eval_jaxpr/ppermute | solution.py:20
  165.3 2.8 fusion.102
  176.5 2.0 multiply_add_fusion.2
  183.9 1.3 dynamic-slice_bitcast_fusion.2
  187.9 9.0 %collective-permute-done.1 = bf16[2,1024,128]{2,1,0:T(8,128)(2,1)S(1)} collective-permute-done((bf16[2,1024,128]{2,1,0:T(8,128)(2,1)}, bf16[2,1024,128]{2,1,0:T(8,128)(2,1)S(1)}, u32[]{:S(2)}, u32[]{:S(2)}) %collective-permute-start.1) | collective-permute-done | bytes 524320 | tf_op jit(solution)/shard_map/while/body/eval_jaxpr/ppermute | solution.py:20
  197.0 10.9 %collective-permute-done = bf16[2,1024,128]{2,1,0:T(8,128)(2,1)} collective-permute-done((bf16[2,1024,128]{2,1,0:T(8,128)(2,1)}, bf16[2,1024,128]{2,1,0:T(8,128)(2,1)}, u32[]{:S(2)}, u32[]{:S(2)}) %collective-permute-start) | collective-permute-done | bytes 524320 | tf_op jit(solution)/shard_map/while/body/eval_jaxpr/ppermute | solution.py:20
  209.1 2.8 fusion.102
  220.4 2.0 multiply_add_fusion.2
  227.8 1.3 dynamic-slice_bitcast_fusion.2
  231.8 9.0 %collective-permute-done.1 = bf16[2,1024,128]{2,1,0:T(8,128)(2,1)S(1)} collective-permute-done((bf16[2,1024,128]{2,1,0:T(8,128)(2,1)}, bf16[2,1024,128]{2,1,0:T(8,128)(2,1)S(1)}, u32[]{:S(2)}, u32[]{:S(2)}) %collective-permute-start.1) | collective-permute-done | bytes 524320 | tf_op jit(solution)/shard_map/while/body/eval_jaxpr/ppermute | solution.py:20
  240.8 10.9 %collective-permute-done = bf16[2,1024,128]{2,1,0:T(8,128)(2,1)} collective-permute-done((bf16[2,1024,128]{2,1,0:T(8,128)(2,1)}, bf16[2,1024,128]{2,1,0:T(8,128)(2,1)}, u32[]{:S(2)}, u32[]{:S(2)}) %collective-permute-start) | collective-permute-done | bytes 524320 | tf_op jit(solution)/shard_map/while/body/eval_jaxpr/ppermute | solution.py:20
  252.9 2.8 fusion.102
  264.2 2.0 multiply_add_fusion.2
  275.6 9.0 %collective-permute-done.1 = bf16[2,1024,128]{2,1,0:T(8,128)(2,1)S(1)} collective-permute-done((bf16[2,1024,128]{2,1,0:T(8,128)(2,1)}, bf16[2,1024,128]{2,1,0:T(8,128)(2,1)S(1)}, u32[]{:S(2)}, u32[]{:S(2)}) %collective-permute-start.1) | collective-permute-done | bytes 524320 | tf_op jit(solution)/shard_map/while/body/eval_jaxpr/ppermute | solution.py:20
  284.7 10.9 %collective-permute-done = bf16[2,1024,128]{2,1,0:T(8,128)(2,1)} collective-permute-done((bf16[2,1024,128]{2,1,0:T(8,128)(2,1)}, bf16[2,1024,128]{2,1,0:T(8,128)(2,1)}, u32[]{:S(2)}, u32[]{:S(2)}) %collective-permute-start) | collective-permute-done | bytes 524320 | tf_op jit(solution)/shard_map/while/body/eval_jaxpr/ppermute | solution.py:20
  296.8 2.8 fusion.102
  308.1 2.0 multiply_add_fusion.2
  (360 shorter events, 123.1 us)
Async XLA Ops:
  7.6 16.9 %collective-permute-start.1 = (bf16[2,1024,128]{2,1,0:T(8,128)(2,1)}, bf16[2,1024,128]{2,1,0:T(8,128)(2,1)S(1)}, u32[]{:S(2)}, u32[]{:S(2)}) collective-permute-start(bf16[2,1024,128]{2,1,0:T(8,128)(2,1)} %broadcast_select_fusion.5), channel_id=1, source_target_pairs={{0,8},{8,16},{16,24},{1,9},{9,17},{17,25},{2,10},{10,18},{18,26},{... | collective-permute-start | bytes 1572872 | tf_op jit(solution)/shard_map/while/body/eval_jaxpr/ppermute | solution.py:20
  9.7 25.0 %collective-permute-start = (bf16[2,1024,128]{2,1,0:T(8,128)(2,1)}, bf16[2,1024,128]{2,1,0:T(8,128)(2,1)}, u32[]{:S(2)}, u32[]{:S(2)}) collective-permute-start(bf16[2,1024,128]{2,1,0:T(8,128)(2,1)} %broadcast_select_fusion.4), channel_id=1, source_target_pairs={{0,8},{8,16},{16,24},{1,9},{9,17},{17,25},{2,10},{10,18},{18,26},{... | collective-permute-start | bytes 1572872 | tf_op jit(solution)/shard_map/while/body/eval_jaxpr/ppermute | solution.py:20
  40.0 1.9 collective-permute-start.4
  41.3 1.7 collective-permute-start.2
  44.4 2.4 collective-permute-start.5
  49.1 16.9 %collective-permute-start.1 = (bf16[2,1024,128]{2,1,0:T(8,128)(2,1)}, bf16[2,1024,128]{2,1,0:T(8,128)(2,1)S(1)}, u32[]{:S(2)}, u32[]{:S(2)}) collective-permute-start(bf16[2,1024,128]{2,1,0:T(8,128)(2,1)} %broadcast_select_fusion.5), channel_id=1, source_target_pairs={{0,8},{8,16},{16,24},{1,9},{9,17},{17,25},{2,10},{10,18},{18,26},{... | collective-permute-start | bytes 1572872 | tf_op jit(solution)/shard_map/while/body/eval_jaxpr/ppermute | solution.py:20
  51.2 25.4 %collective-permute-start = (bf16[2,1024,128]{2,1,0:T(8,128)(2,1)}, bf16[2,1024,128]{2,1,0:T(8,128)(2,1)}, u32[]{:S(2)}, u32[]{:S(2)}) collective-permute-start(bf16[2,1024,128]{2,1,0:T(8,128)(2,1)} %broadcast_select_fusion.4), channel_id=1, source_target_pairs={{0,8},{8,16},{16,24},{1,9},{9,17},{17,25},{2,10},{10,18},{18,26},{... | collective-permute-start | bytes 1572872 | tf_op jit(solution)/shard_map/while/body/eval_jaxpr/ppermute | solution.py:20
  81.9 1.9 collective-permute-start.4
  83.2 1.7 collective-permute-start.2
  86.3 2.4 collective-permute-start.5
  92.0 17.2 %collective-permute-start.1 = (bf16[2,1024,128]{2,1,0:T(8,128)(2,1)}, bf16[2,1024,128]{2,1,0:T(8,128)(2,1)S(1)}, u32[]{:S(2)}, u32[]{:S(2)}) collective-permute-start(bf16[2,1024,128]{2,1,0:T(8,128)(2,1)} %broadcast_select_fusion.5), channel_id=1, source_target_pairs={{0,8},{8,16},{16,24},{1,9},{9,17},{17,25},{2,10},{10,18},{18,26},{... | collective-permute-start | bytes 1572872 | tf_op jit(solution)/shard_map/while/body/eval_jaxpr/ppermute | solution.py:20
  94.2 26.0 %collective-permute-start = (bf16[2,1024,128]{2,1,0:T(8,128)(2,1)}, bf16[2,1024,128]{2,1,0:T(8,128)(2,1)}, u32[]{:S(2)}, u32[]{:S(2)}) collective-permute-start(bf16[2,1024,128]{2,1,0:T(8,128)(2,1)} %broadcast_select_fusion.4), channel_id=1, source_target_pairs={{0,8},{8,16},{16,24},{1,9},{9,17},{17,25},{2,10},{10,18},{18,26},{... | collective-permute-start | bytes 1572872 | tf_op jit(solution)/shard_map/while/body/eval_jaxpr/ppermute | solution.py:20
  125.5 1.9 collective-permute-start.4
  126.8 1.7 collective-permute-start.2
  129.9 2.4 collective-permute-start.5
  135.6 17.5 %collective-permute-start.1 = (bf16[2,1024,128]{2,1,0:T(8,128)(2,1)}, bf16[2,1024,128]{2,1,0:T(8,128)(2,1)S(1)}, u32[]{:S(2)}, u32[]{:S(2)}) collective-permute-start(bf16[2,1024,128]{2,1,0:T(8,128)(2,1)} %broadcast_select_fusion.5), channel_id=1, source_target_pairs={{0,8},{8,16},{16,24},{1,9},{9,17},{17,25},{2,10},{10,18},{18,26},{... | collective-permute-start | bytes 1572872 | tf_op jit(solution)/shard_map/while/body/eval_jaxpr/ppermute | solution.py:20
  137.7 26.3 %collective-permute-start = (bf16[2,1024,128]{2,1,0:T(8,128)(2,1)}, bf16[2,1024,128]{2,1,0:T(8,128)(2,1)}, u32[]{:S(2)}, u32[]{:S(2)}) collective-permute-start(bf16[2,1024,128]{2,1,0:T(8,128)(2,1)} %broadcast_select_fusion.4), channel_id=1, source_target_pairs={{0,8},{8,16},{16,24},{1,9},{9,17},{17,25},{2,10},{10,18},{18,26},{... | collective-permute-start | bytes 1572872 | tf_op jit(solution)/shard_map/while/body/eval_jaxpr/ppermute | solution.py:20
  169.3 1.9 collective-permute-start.4
  170.6 1.7 collective-permute-start.2
  173.7 2.4 collective-permute-start.5
  179.4 17.5 %collective-permute-start.1 = (bf16[2,1024,128]{2,1,0:T(8,128)(2,1)}, bf16[2,1024,128]{2,1,0:T(8,128)(2,1)S(1)}, u32[]{:S(2)}, u32[]{:S(2)}) collective-permute-start(bf16[2,1024,128]{2,1,0:T(8,128)(2,1)} %broadcast_select_fusion.5), channel_id=1, source_target_pairs={{0,8},{8,16},{16,24},{1,9},{9,17},{17,25},{2,10},{10,18},{18,26},{... | collective-permute-start | bytes 1572872 | tf_op jit(solution)/shard_map/while/body/eval_jaxpr/ppermute | solution.py:20
  181.6 26.3 %collective-permute-start = (bf16[2,1024,128]{2,1,0:T(8,128)(2,1)}, bf16[2,1024,128]{2,1,0:T(8,128)(2,1)}, u32[]{:S(2)}, u32[]{:S(2)}) collective-permute-start(bf16[2,1024,128]{2,1,0:T(8,128)(2,1)} %broadcast_select_fusion.4), channel_id=1, source_target_pairs={{0,8},{8,16},{16,24},{1,9},{9,17},{17,25},{2,10},{10,18},{18,26},{... | collective-permute-start | bytes 1572872 | tf_op jit(solution)/shard_map/while/body/eval_jaxpr/ppermute | solution.py:20
  213.2 1.9 collective-permute-start.4
  217.6 2.4 collective-permute-start.5
  223.3 17.5 %collective-permute-start.1 = (bf16[2,1024,128]{2,1,0:T(8,128)(2,1)}, bf16[2,1024,128]{2,1,0:T(8,128)(2,1)S(1)}, u32[]{:S(2)}, u32[]{:S(2)}) collective-permute-start(bf16[2,1024,128]{2,1,0:T(8,128)(2,1)} %broadcast_select_fusion.5), channel_id=1, source_target_pairs={{0,8},{8,16},{16,24},{1,9},{9,17},{17,25},{2,10},{10,18},{18,26},{... | collective-permute-start | bytes 1572872 | tf_op jit(solution)/shard_map/while/body/eval_jaxpr/ppermute | solution.py:20
  225.4 26.3 %collective-permute-start = (bf16[2,1024,128]{2,1,0:T(8,128)(2,1)}, bf16[2,1024,128]{2,1,0:T(8,128)(2,1)}, u32[]{:S(2)}, u32[]{:S(2)}) collective-permute-start(bf16[2,1024,128]{2,1,0:T(8,128)(2,1)} %broadcast_select_fusion.4), channel_id=1, source_target_pairs={{0,8},{8,16},{16,24},{1,9},{9,17},{17,25},{2,10},{10,18},{18,26},{... | collective-permute-start | bytes 1572872 | tf_op jit(solution)/shard_map/while/body/eval_jaxpr/ppermute | solution.py:20
  257.0 1.9 collective-permute-start.4
  261.4 2.4 collective-permute-start.5
  267.1 17.5 %collective-permute-start.1 = (bf16[2,1024,128]{2,1,0:T(8,128)(2,1)}, bf16[2,1024,128]{2,1,0:T(8,128)(2,1)S(1)}, u32[]{:S(2)}, u32[]{:S(2)}) collective-permute-start(bf16[2,1024,128]{2,1,0:T(8,128)(2,1)} %broadcast_select_fusion.5), channel_id=1, source_target_pairs={{0,8},{8,16},{16,24},{1,9},{9,17},{17,25},{2,10},{10,18},{18,26},{... | collective-permute-start | bytes 1572872 | tf_op jit(solution)/shard_map/while/body/eval_jaxpr/ppermute | solution.py:20
  269.2 26.3 %collective-permute-start = (bf16[2,1024,128]{2,1,0:T(8,128)(2,1)}, bf16[2,1024,128]{2,1,0:T(8,128)(2,1)}, u32[]{:S(2)}, u32[]{:S(2)}) collective-permute-start(bf16[2,1024,128]{2,1,0:T(8,128)(2,1)} %broadcast_select_fusion.4), channel_id=1, source_target_pairs={{0,8},{8,16},{16,24},{1,9},{9,17},{17,25},{2,10},{10,18},{18,26},{... | collective-permute-start | bytes 1572872 | tf_op jit(solution)/shard_map/while/body/eval_jaxpr/ppermute | solution.py:20
  300.9 1.9 collective-permute-start.4
  305.2 2.4 collective-permute-start.5
  (20 other events, 176.3 us)
where the time goes:
time: 315 us; the launch traced here: 310 us
  waiting for transfers between devices  140 us (44%)
  other arithmetic  69.4 us (22%)
  matrix products  33.5 us (11%)
  local copies, waits for them, and re-layouts  28.1 us (9%)
  starting transfers between devices  26.8 us (9%)
  loops' own time  9.79 us (3%)
    ppermute x14, waiting for transfers between devices, from_behind(): return lax.ppermute(value, axis, pairs)  136 us
    dot_general x112, matrix products, blockwise(): return jnp.einsum(form, matrix, vector, preferred_element_type=jnp.float32)  30.7 us
    slice x7, other arithmetic, complex_apply(): parts[1]  19.9 us
    ppermute x14, starting transfers between devices, from_behind(): return lax.ppermute(value, axis, pairs)  17.9 us
    add x7, other arithmetic, segment(): gradient = gradient.at[0].add(weight * correlation)  13.2 us
    while x14, other arithmetic  11.8 us
    another operation x1, loops' own time, per_device(): final = lax.fori_loop(0, freqs + sections - 1, segment, start)  9.79 us
    dynamic_slice x14, local copies, waits for them, and re-layouts, segment(): lax.dynamic_index_in_dim(sources, freq_index, 0, keepdims=False)  9.58 us
  transfers between devices with their start and end apart: 42, of which 28 were waited for; matrix products, arithmetic and copies ran while one was open for 19% of the time, Pallas kernels for 0%

commit v1 on v0

v1 whole, which is shorter than its diff:
```python
import functools
import math

import jax
import jax.numpy as jnp
from jax import lax
from jax.experimental import pallas as pl
from jax.experimental.pallas import tpu as pltpu
from jax.sharding import PartitionSpec as P

MESH = pl.DeviceIdType.MESH
F32 = jnp.float32
BF16 = jnp.bfloat16

SIN_TERMS = [(-1.0) ** k / math.factorial(2 * k + 1) for k in range(7)]
COS_TERMS = [(-1.0) ** k / math.factorial(2 * k) for k in range(8)]
PI_HIGH = 3.140625
PI_MID = 9.67502593994140625e-4
PI_LOW = math.pi - PI_HIGH - PI_MID


def series(square, terms):
    total = jnp.full_like(square, terms[-1])
    for term in terms[-2::-1]:
        total = total * square + term
    return total


def sincos(angle):
    turns = jnp.floor(angle * (1.0 / math.pi) + 0.5)
    rest = ((angle - turns * PI_HIGH) - turns * PI_MID) - turns * PI_LOW
    odd = turns - 2.0 * jnp.floor(turns * 0.5)
    sign = 1.0 - 2.0 * odd
    square = rest * rest
    return series(square, SIN_TERMS) * (rest * sign), series(square, COS_TERMS) * sign


def block_form(blocks):
    k_real, k_imag = blocks[0], blocks[1]
    top = jnp.concatenate([k_real, -k_imag], axis=1)
    bottom = jnp.concatenate([k_imag, k_real], axis=1)
    return jnp.concatenate([top, bottom], axis=0)


def kernel(
    sections, pair, rows, recv_in, amp, src_x, src_y, omegas, slow_in, table_in, zones,
    out, slow, rec, wave, table, zone_buf, zone_rows, rotated, inline, own, sent, got, total,
    local_sems, zone_send, zone_recv, slow_send, slow_recv, fwd_send, fwd_recv,
    rec_send, rec_recv, swap_send, swap_recv, grad_send, grad_recv,
):
    d = lax.axis_index("depth")
    line = lax.axis_index("xline")
    q = lax.rem(line, pair)
    block = line // pair
    mate_line = line + 1 - 2 * q
    width = recv_in.shape[3]
    order = pair * width
    slots = wave.shape[0]
    mine = pl.ds(pl.multiple_of(q * width, width), width)
    theirs = pl.ds(pl.multiple_of((1 - q) * width, width), width)

    def rows_of(section):
        return pl.ds(pl.multiple_of(section * order, order), order)

    barrier = pltpu.get_barrier_semaphore()
    pl.semaphore_signal(barrier, inc=1, device_id=(d, mate_line), device_id_type=MESH)
    others = [lax.rem(d + k, sections) for k in range(1, sections)]
    for other in others:
        pl.semaphore_signal(barrier, inc=1, device_id=(other, line), device_id_type=MESH)

    freqs = pl.ds(q * slots, slots)
    local = [
        pltpu.make_async_copy(
            slow_in.at[0, rows_of(d), :], slow.at[d, :, mine], local_sems.at[0]
        ),
        pltpu.make_async_copy(
            recv_in.at[freqs, :, rows_of(d), :], rec.at[:, :, :, mine], local_sems.at[1]
        ),
        pltpu.make_async_copy(table_in.at[freqs], table, local_sems.at[2]),
        pltpu.make_async_copy(zones, zone_buf.at[d], local_sems.at[3]),
    ]
    for copy in local:
        copy.start()
    pl.semaphore_wait(barrier, sections)

    zone_copies, slow_copies = [], []
    for k, other in enumerate(others):
        zone_copies.append(
            pltpu.make_async_remote_copy(
                src_ref=zones, dst_ref=zone_buf.at[d], send_sem=zone_send.at[k],
                recv_sem=zone_recv.at[d], device_id=(other, line), device_id_type=MESH,
            )
        )
        slow_copies.append(
            pltpu.make_async_remote_copy(
                src_ref=slow_in.at[0, rows_of(other), :], dst_ref=slow.at[d, :, mine],
                send_sem=slow_send.at[k], recv_sem=slow_recv.at[d],
                device_id=(other, line), device_id_type=MESH,
            )
        )
    for copy in zone_copies + slow_copies:
        copy.start()
    rec_copy = pltpu.make_async_remote_copy(
        src_ref=recv_in.at[pl.ds((1 - q) * slots, slots), :, rows_of(d), :],
        dst_ref=rec.at[:, :, :, mine], send_sem=rec_send, recv_sem=rec_recv,
        device_id=(d, mate_line), device_id_type=MESH,
    )
    rec_copy.start()

    points = src_x.shape[1]
    cells = lax.broadcasted_iota(jnp.int32, (order, points), 0)
    hit_x = cells + d * order == src_x[...]
    hit_y = jnp.where(cells + block * order == src_y[...], 1.0, 0.0).astype(BF16)
    for slot in range(slots):
        for part in range(2):
            amps = amp[q * slots + slot, pl.ds(part, 1), :].astype(F32)
            spread = jnp.where(hit_x, amps, 0.0).astype(BF16)
            field = lax.dot_general(
                spread, hit_y, (((1,), (1,)), ((), ())), preferred_element_type=F32
            )
            wave[slot, 0, part] = field.astype(BF16)

    def arrived_slow(level):
        return pltpu.make_async_remote_copy(
            src_ref=slow.at[level, :, mine], dst_ref=slow.at[level, :, mine],
            send_sem=slow_send.at[0], recv_sem=slow_recv.at[level],
            device_id=(d, mate_line), device_id_type=MESH,
        )

    def forward(level, half):
        return pltpu.make_async_remote_copy(
            src_ref=slow.at[level, :, half], dst_ref=slow.at[level, :, half],
            send_sem=fwd_send.at[level], recv_sem=fwd_recv.at[level],
            device_id=(d, mate_line), device_id_type=MESH,
        )

    local[0].wait()

    def relay(level):
        @pl.when(level != d)
        def _():
            arrived_slow(level).wait_recv()

        forward(level, mine).start()

    relay(0)

    local[1].wait()
    rec_copy.wait_recv()
    for slot in range(slots):
        wave[slot, 1, 0] = rec[slot, 0]
        wave[slot, 1, 1] = -rec[slot, 1]
    local[2].wait()
    local[3].wait()
    for level in range(sections):
        @pl.when(level != d)
        def _():
            pltpu.make_async_remote_copy(
                src_ref=zones, dst_ref=zone_buf.at[level], send_sem=zone_send.at[0],
                recv_sem=zone_recv.at[level], device_id=(d, mate_line), device_id_type=MESH,
            ).wait_recv()
    zone_copy = pltpu.make_async_copy(zone_buf, zone_rows, local_sems.at[4])
    zone_copy.start()
    zone_copy.wait()
    forward(0, theirs).wait_recv()

    def advance(level, slot):
        omega = omegas[q * slots + slot]
        m_x = block_form(table[slot, zone_rows[level, 0, d]])
        m_y = block_form(table[slot, zone_rows[level, 0, sections + block]])
        step = min(rows, order)
        for start in range(0, order, step):
            part = slice(start, start + step)
            sine, cosine = sincos(omega * slow[level, part, :])
            for field in range(2):
                real = wave[slot, field, 0, part, :].astype(F32)
                imag = wave[slot, field, 1, part, :].astype(F32)
                lanes = slice(field * order, (field + 1) * order)
                rotated[part, lanes] = (real * cosine - imag * sine).astype(BF16)
                rotated[order + start:order + start + step, lanes] = (
                    real * sine + imag * cosine
                ).astype(BF16)
        for field in range(2):
            lanes = slice(field * order, (field + 1) * order)
            value = rotated[:, lanes]
            solved = value.astype(F32) + jnp.dot(m_x, value, preferred_element_type=F32)
            solved = solved.astype(BF16)
            inline[lanes, 0:order] = solved[:order]
            inline[lanes, order:] = solved[order:]
        value = inline[...]
        product = []
        for part in range(2):
            lanes = slice(part * order, (part + 1) * order)
            solved = value[:, lanes].astype(F32) + lax.dot_general(
                value, m_y[lanes], (((1,), (1,)), ((), ())), preferred_element_type=F32
            )
            solved = solved.astype(BF16)
            wave[slot, 0, part] = solved[:order]
            wave[slot, 1, part] = solved[order:]
            product.append(solved[:order].astype(F32) * solved[order:].astype(F32))
        image = (omega * omega) * (product[0] - product[1])
        if slot == 0:
            total[...] = image
        else:
            total[...] += image

    def swap(level):
        return pltpu.make_async_remote_copy(
            src_ref=sent.at[level], dst_ref=got.at[level],
            send_sem=swap_send.at[level], recv_sem=swap_recv.at[level],
            device_id=(d, mate_line), device_id_type=MESH,
        )

    def deliver_copy(level):
        return pltpu.make_async_remote_copy(
            src_ref=own.at[level], dst_ref=out.at[rows_of(d), :],
            send_sem=grad_send.at[level], recv_sem=grad_recv.at[d],
            device_id=(level, line), device_id_type=MESH,
        )

    def deliver(level):
        swap(level).wait_recv()
        both = own[level].astype(F32) + got[level].astype(F32)

        @pl.when(level == d)
        def _():
            out[rows_of(d), :] = both.astype(BF16)

        @pl.when(level != d)
        def _():
            own[level] = both.astype(BF16)
            deliver_copy(level).start()

    def level_step(level, carry):
        for slot in range(slots):
            advance(level, slot)
            if slot == 0:
                @pl.when(level + 1 < sections)
                def _():
                    relay(level + 1)

                @pl.when(level > 0)
                def _():
                    deliver(level - 1)
        own[level] = total[:, mine].astype(BF16)
        sent[level] = total[:, theirs].astype(BF16)
        swap(level).start()

        @pl.when(level + 1 < sections)
        def _():
            forward(level + 1, theirs).wait_recv()

        return carry

    lax.fori_loop(0, sections, level_step, 0)
    deliver(sections - 1)

    for copy in zone_copies + slow_copies:
        copy.wait_send()
    rec_copy.wait_send()
    for level in range(sections):
        forward(level, mine).wait_send()
        swap(level).wait_send()

        @pl.when(level != d)
        def _():
            deliver_copy(level).wait_send()
            pltpu.make_async_remote_copy(
                src_ref=own.at[level], dst_ref=out.at[rows_of(level), :],
                send_sem=grad_send.at[0], recv_sem=grad_recv.at[level],
                device_id=(level, line), device_id_type=MESH,
            ).wait_recv()


def per_device(
    receiver_data, source_amp, source_x, source_y, omegas, slowness, inverses, zones_x, zones_y
):
    sections = lax.axis_size("depth")
    freqs, _, width_x, width_y = receiver_data.shape
    order = inverses.shape[-1]
    pair = order // width_y
    points = source_x.shape[0]
    zone_count = inverses.shape[1]
    slots = freqs // pair
    assert pair == 2 and width_x == order * sections and slowness.shape[0] == 1
    zones = jnp.concatenate([zones_x, zones_y], axis=1)
    zones = jnp.pad(zones, ((0, 0), (0, 128 - zones.shape[1])))
    vmem = pl.BlockSpec(memory_space=pltpu.VMEM)
    smem = pl.BlockSpec(memory_space=pltpu.SMEM)
    anywhere = pl.BlockSpec(memory_space=pl.ANY)
    dma = pltpu.SemaphoreType.DMA
    out = pl.pallas_call(
        functools.partial(kernel, sections, pair, 32),
        out_shape=jax.ShapeDtypeStruct((width_x, width_y), BF16),
        in_specs=[anywhere, vmem, vmem, vmem, smem, anywhere, anywhere, vmem],
        out_specs=vmem,
        scratch_shapes=[
            pltpu.VMEM((sections, order, order), slowness.dtype),
            pltpu.VMEM((slots, 2, order, order), BF16),
            pltpu.VMEM((slots, 2, 2, order, order), BF16),
            pltpu.VMEM((slots, zone_count, 2, order, order), BF16),
            pltpu.VMEM((sections, 1, 128), jnp.int32),
            pltpu.SMEM((sections, 1, 128), jnp.int32),
            pltpu.VMEM((2 * order, 2 * order), BF16),
            pltpu.VMEM((2 * order, 2 * order), BF16),
            pltpu.VMEM((sections, order, width_y), BF16),
            pltpu.VMEM((sections, order, width_y), BF16),
            pltpu.VMEM((sections, order, width_y), BF16),
            pltpu.VMEM((order, order), F32),
            dma((5,)),
            dma((sections,)), dma((sections,)),
            dma((sections,)), dma((sections,)),
            dma((sections,)), dma((sections,)),
            dma, dma,
            dma((sections,)), dma((sections,)),
            dma((sections,)), dma((sections,)),
        ],
        compiler_params=pltpu.CompilerParams(collective_id=0, has_side_effects=True),
    )(
        receiver_data, source_amp, source_x.reshape(1, points), source_y.reshape(1, points),
        omegas, slowness, inverses, zones,
    )
    return out.astype(F32)[None]


def solution(mesh):
    in_specs = (
        P(None, None, None, "xline"),
        P(),
        P(),
        P(),
        P(),
        P("depth", None, "xline"),
        P(),
        P("depth", None),
        P("depth", None),
    )
    out_specs = P("depth", None, "xline")
    return jax.shard_map(
        per_device, mesh=mesh, in_specs=in_specs, out_specs=out_specs, check_vma=False
    )
```

time: 315 us -> 29.4 us (0.09); the launches traced: 310 us -> 29.2 us
  waiting for transfers between devices: 140 us -> 0 us
  other arithmetic: 69.4 us -> 2.52 us
  matrix products: 33.5 us -> 0 us
  local copies, waits for them, and re-layouts: 28.1 us -> 0.52 us
  starting transfers between devices: 26.8 us -> 0 us
  Pallas kernels: 0 us -> 26.2 us
  loops' own time: 9.79 us -> 0 us
    ppermute x42 -> x0, waiting for transfers between devices: 140 us -> none  [the longest x14 136 us: from_behind(): return lax.ppermute(value, axis, pairs)]
    dot_general x113 -> x0, matrix products: 33.5 us -> none  [the longest x112 30.7 us: blockwise(): return jnp.einsum(form, matrix, vector, preferred_element_type=jnp.float32)]
    ppermute x42 -> x0, starting transfers between devices: 26.8 us -> none  [the longest x14 17.9 us: from_behind(): return lax.ppermute(value, axis, pairs)]
    pallas_call x0 -> x1, Pallas kernels: none -> 26.2 us  [per_device(): pl.pallas_call(functools.partial(kernel, sections, pair, 32), out_shape=j...]
    select_n x63 -> x0, other arithmetic: 21.7 us -> none  [the longest x7 8.8 us: segment(): jnp.where(first, lax.dynamic_index_in_dim(receiver_data, freq_index, 0, k...]
    slice x7 -> x0, other arithmetic: 19.9 us -> none  [complex_apply(): parts[1]]
    dynamic_slice x22 -> x0, local copies, waits for them, and re-layouts: 14.1 us -> none  [the longest x14 9.58 us: segment(): lax.dynamic_index_in_dim(sources, freq_index, 0, keepdims=False)]
    add x7 -> x0, other arithmetic: 13.2 us -> none  [segment(): gradient = gradient.at[0].add(weight * correlation)]
  transfers between devices with their start and end apart: 42 -> 0, of which waited for: 28 -> 0; matrix products, arithmetic and copies ran while one was open for 19% -> 0% of each run, Pallas kernels for 0% -> 0%
where the time goes in v1:
time: 29.4 us; the launch traced here: 29.2 us
  Pallas kernels  26.2 us (89%)
  other arithmetic  2.52 us (9%)
  local copies, waits for them, and re-layouts  0.52 us (2%)
    pallas_call x1, Pallas kernels, per_device(): pl.pallas_call(functools.partial(kernel, sections, pair, 32), out_shape=j...  26.2 us
    broadcast_in_dim x1, other arithmetic, per_device(): return out.astype(F32)[None]  1.78 us
    concatenate x1, other arithmetic, per_device(): zones = jnp.concatenate([zones_x, zones_y], axis=1)  0.75 us

profile of v1, /device:TPU:6, one launch (start us, length us, event | category | flops | bytes accessed | tf_op | source)
XLA Modules:
  0.0 29.2 jit_solution(12608905726877214102)
XLA Ops:
  0.0 0.7 %pad_add_fusion = s32[1,8]{1,0:T(1,128)S(1)} fusion(s32[1,4]{1,0:T(1,128)} %param.17, s32[1,4]{1,0:T(1,128)} %param.16), kind=kLoop, calls=%fused_computation.1 | loop fusion | flops 8 | bytes 64 | tf_op jit(solution)/shard_map/concatenate | solution.py:286
  0.7 0.5 %pad.4.zones = s32[1,128]{1,0:T(1,128)} pad(s32[1,8]{1,0:T(1,128)S(1)} %pad_add_fusion, s32[]{:T(128)} %constant.0.clone.1), padding=0_0x0_120 | pad | bytes 548 | tf_op jit(solution)/shard_map/jit(_pad)/pad | solution.py:287
  1.3 26.2 %shard_map.91 = bf16[1024,128]{1,0:T(8,128)(2,1)} custom-call(bf16[4,2,1024,128]{3,2,1,0:T(8,128)(2,1)} %recv_in.1, bf16[4,2,256]{2,1,0:T(2,128)(2,1)} %amp.1, s32[1,256]{1,0:T(1,128)} %bitcast.5, s32[1,256]{1,0:T(1,128)} %bitcast.6, f32[4]{0:T(128)} %omegas.1, f32[1,1024,128]{2,1,0:T(8,128)} %slow_in.1, bf16[4,4,2,256,256]{4,3,2,1,0:T(8,128)(2,1)} %table_in.1, ...), custom_call_target="tpu_custom_call" | custom-call | tf_op jit(solution)/shard_map/pallas_call | solution.py:292
  27.5 1.8 %bitcast_convert_fusion = f32[1,1024,128]{2,1,0:T(8,128)} fusion(bf16[1024,128]{1,0:T(8,128)(2,1)} %shard_map.91), kind=kLoop, calls=%fused_computation | loop fusion | flops 131072 | bytes 786432 | tf_op jit(solution)/shard_map/broadcast_in_dim | solution.py:323

commit v2 on v1

--- a/solution.py
+++ b/solution.py
@@ -3,6 +3,7 @@
 
 import jax
 import jax.numpy as jnp
+import numpy as np
 from jax import lax
 from jax.experimental import pallas as pl
 from jax.experimental.pallas import tpu as pltpu
@@ -12,27 +13,37 @@
 F32 = jnp.float32
 BF16 = jnp.bfloat16
 
-SIN_TERMS = [(-1.0) ** k / math.factorial(2 * k + 1) for k in range(7)]
-COS_TERMS = [(-1.0) ** k / math.factorial(2 * k) for k in range(8)]
-PI_HIGH = 3.140625
-PI_MID = 9.67502593994140625e-4
-PI_LOW = math.pi - PI_HIGH - PI_MID
+SLOW_LOW, SLOW_HIGH = 0.2, 2.0
+OMEGA_LOW, OMEGA_HIGH = 0.5, 3.0
+SLOW_MID = 0.5 * (SLOW_LOW + SLOW_HIGH)
+CODE_STEP = (SLOW_HIGH - SLOW_LOW) / 65532.0
+HALF_SPAN = 0.5 * max(OMEGA_HIGH * SLOW_HIGH - math.pi, math.pi - OMEGA_LOW * SLOW_LOW) + 0.01
+
+
+def fitted(function, count):
+    nodes = np.cos(np.pi * (np.arange(64) + 0.5) / 64)
+    square = 0.5 * HALF_SPAN**2 * (nodes + 1.0)
+    fit = np.polynomial.Chebyshev.fit(square, function(np.sqrt(square)), count - 1)
+    return [float(term) for term in fit.convert(kind=np.polynomial.Polynomial).coef]
+
+
+SIN_TERMS = fitted(lambda t: np.sin(t) / t, 6)
+COS_TERMS = fitted(np.cos, 6)
 
 
 def series(square, terms):
-    total = jnp.full_like(square, terms[-1])
-    for term in terms[-2::-1]:
+    total = square * terms[-1] + terms[-2]
+    for term in terms[-3::-1]:
         total = total * square + term
     return total
 
 
-def sincos(angle):
-    turns = jnp.floor(angle * (1.0 / math.pi) + 0.5)
-    rest = ((angle - turns * PI_HIGH) - turns * PI_MID) - turns * PI_LOW
-    odd = turns - 2.0 * jnp.floor(turns * 0.5)
-    sign = 1.0 - 2.0 * odd
-    square = rest * rest
-    return series(square, SIN_TERMS) * (rest * sign), series(square, COS_TERMS) * sign
+def sincos(half):
+    square = half * half
+    sine = series(square, SIN_TERMS) * half
+    cosine = series(square, COS_TERMS)
+    double = sine + sine
+    return -(double * cosine), double * sine - 1.0
 
 
 def block_form(blocks):
@@ -43,8 +54,10 @@
 
 
 def kernel(
-    sections, pair, rows, recv_in, amp, src_x, src_y, omegas, slow_in, table_in, zones,
-    out, slow, rec, wave, table, zone_buf, zone_rows, rotated, inline, own, sent, got, total,
+    sections, pair, rows, recv_in, amp, src_x, src_y, omegas, slow_in, table_in,
+    zones_x, zones_y,
+    out, slow, slow_raw, code, rec, wave, table, zones, zone_buf, zone_rows, trig, rotated, inline,
+    own, sent, got, total,
     local_sems, zone_send, zone_recv, slow_send, slow_recv, fwd_send, fwd_recv,
     rec_send, rec_recv, swap_send, swap_recv, grad_send, grad_recv,
 ):
@@ -71,16 +84,25 @@
     freqs = pl.ds(q * slots, slots)
     local = [
         pltpu.make_async_copy(
-            slow_in.at[0, rows_of(d), :], slow.at[d, :, mine], local_sems.at[0]
+            slow_in.at[0], slow_raw, local_sems.at[0]
         ),
         pltpu.make_async_copy(
             recv_in.at[freqs, :, rows_of(d), :], rec.at[:, :, :, mine], local_sems.at[1]
         ),
         pltpu.make_async_copy(table_in.at[freqs], table, local_sems.at[2]),
-        pltpu.make_async_copy(zones, zone_buf.at[d], local_sems.at[3]),
     ]
     for copy in local:
         copy.start()
+    zones[...] = jnp.zeros_like(zones)
+    zones[0:1, 0:zones_x.shape[1]] = zones_x[...]
+    zones[1:2, 0:zones_y.shape[1]] = zones_y[...]
+    zone_buf[d] = zones[...]
+    local[0].wait()
+    for start in range(0, slow_raw.shape[0], order):
+        part = slice(start, start + order)
+        scaled = (slow_raw[part, :] - SLOW_MID) * (1.0 / CODE_STEP)
+        code[part, :] = jnp.round(scaled).astype(jnp.int32).astype(jnp.int16)
+    slow[d, :, mine] = code[rows_of(d), :]
     pl.semaphore_wait(barrier, sections)
 
     zone_copies, slow_copies = [], []
@@ -93,7 +115,7 @@
         )
         slow_copies.append(
             pltpu.make_async_remote_copy(
-                src_ref=slow_in.at[0, rows_of(other), :], dst_ref=slow.at[d, :, mine],
+                src_ref=code.at[rows_of(other), :], dst_ref=slow.at[d, :, mine],
                 send_sem=slow_send.at[k], recv_sem=slow_recv.at[d],
                 device_id=(other, line), device_id_type=MESH,
             )
@@ -134,8 +156,6 @@
             device_id=(d, mate_line), device_id_type=MESH,
         )
 
-    local[0].wait()
-
     def relay(level):
         @pl.when(level != d)
         def _():
@@ -151,7 +171,6 @@
         wave[slot, 1, 0] = rec[slot, 0]
         wave[slot, 1, 1] = -rec[slot, 1]
     local[2].wait()
-    local[3].wait()
     for level in range(sections):
         @pl.when(level != d)
         def _():
@@ -159,35 +178,49 @@
                 src_ref=zones, dst_ref=zone_buf.at[level], send_sem=zone_send.at[0],
                 recv_sem=zone_recv.at[level], device_id=(d, mate_line), device_id_type=MESH,
             ).wait_recv()
-    zone_copy = pltpu.make_async_copy(zone_buf, zone_rows, local_sems.at[4])
+    zone_copy = pltpu.make_async_copy(zone_buf, zone_rows, local_sems.at[3])
     zone_copy.start()
     zone_copy.wait()
     forward(0, theirs).wait_recv()
 
-    def advance(level, slot):
+    def turn(level, slot):
         omega = omegas[q * slots + slot]
-        m_x = block_form(table[slot, zone_rows[level, 0, d]])
-        m_y = block_form(table[slot, zone_rows[level, 0, sections + block]])
-        step = min(rows, order)
-        for start in range(0, order, step):
-            part = slice(start, start + step)
-            sine, cosine = sincos(omega * slow[level, part, :])
+        slope = omega * (0.5 * CODE_STEP)
+        shift = omega * (0.5 * SLOW_MID) - 0.5 * math.pi
+        for start in range(0, order, rows):
+            part = slice(start, start + rows)
+            value = slow[level, part, :].astype(jnp.int32).astype(F32)
+            sine, cosine = sincos(value * slope + shift)
+            trig[level % 2, slot, 0, part, :] = sine
+            trig[level % 2, slot, 1, part, :] = cosine
+
+    def rotate(level, slot):
+        for start in range(0, order, rows):
+            part = slice(start, start + rows)
+            sine, cosine = trig[level % 2, slot, 0, part, :], trig[level % 2, slot, 1, part, :]
             for field in range(2):
                 real = wave[slot, field, 0, part, :].astype(F32)
                 imag = wave[slot, field, 1, part, :].astype(F32)
                 lanes = slice(field * order, (field + 1) * order)
-                rotated[part, lanes] = (real * cosine - imag * sine).astype(BF16)
-                rotated[order + start:order + start + step, lanes] = (
+                rotated[slot, part, lanes] = (real * cosine - imag * sine).astype(BF16)
+                rotated[slot, order + start:order + start + rows, lanes] = (
                     real * sine + imag * cosine
                 ).astype(BF16)
+
+    def solve_inline(level, slot):
+        m_x = block_form(table[slot, zone_rows[level, 0, d]])
         for field in range(2):
             lanes = slice(field * order, (field + 1) * order)
-            value = rotated[:, lanes]
+            value = rotated[slot, :, lanes]
             solved = value.astype(F32) + jnp.dot(m_x, value, preferred_element_type=F32)
             solved = solved.astype(BF16)
-            inline[lanes, 0:order] = solved[:order]
-            inline[lanes, order:] = solved[order:]
-        value = inline[...]
+            inline[slot, lanes, 0:order] = solved[:order]
+            inline[slot, lanes, order:] = solved[order:]
+
+    def solve_crossline(level, slot):
+        omega = omegas[q * slots + slot]
+        m_y = block_form(table[slot, zone_rows[level, 1, block]])
+        value = inline[slot]
         product = []
         for part in range(2):
             lanes = slice(part * order, (part + 1) * order)
@@ -231,28 +264,27 @@
             own[level] = both.astype(BF16)
             deliver_copy(level).start()
 
-    def level_step(level, carry):
-        for slot in range(slots):
-            advance(level, slot)
-            if slot == 0:
-                @pl.when(level + 1 < sections)
-                def _():
-                    relay(level + 1)
-
-                @pl.when(level > 0)
-                def _():
-                    deliver(level - 1)
+    for level in range(sections):
+        if level + 1 < sections:
+            relay(level + 1)
+            if level > 0:
+                forward(level + 1, theirs).wait_recv()
+        if level > 0:
+            deliver(level - 1)
+        if level < 2:
+            for slot in range(slots):
+                turn(level, slot)
+        for stage in (rotate, solve_inline, solve_crossline):
+            for slot in range(slots):
+                stage(level, slot)
+        if 0 < level < sections - 1:
+            for slot in range(slots):
+                turn(level + 1, slot)
         own[level] = total[:, mine].astype(BF16)
         sent[level] = total[:, theirs].astype(BF16)
         swap(level).start()
-
-        @pl.when(level + 1 < sections)
-        def _():
-            forward(level + 1, theirs).wait_recv()
-
-        return carry
-
-    lax.fori_loop(0, sections, level_step, 0)
+        if level == 0:
+            forward(1, theirs).wait_recv()
     deliver(sections - 1)
 
     for copy in zone_copies + slow_copies:
@@ -283,8 +315,6 @@
     zone_count = inverses.shape[1]
     slots = freqs // pair
     assert pair == 2 and width_x == order * sections and slowness.shape[0] == 1
-    zones = jnp.concatenate([zones_x, zones_y], axis=1)
-    zones = jnp.pad(zones, ((0, 0), (0, 128 - zones.shape[1])))
     vmem = pl.BlockSpec(memory_space=pltpu.VMEM)
     smem = pl.BlockSpec(memory_space=pltpu.SMEM)
     anywhere = pl.BlockSpec(memory_space=pl.ANY)
@@ -292,22 +322,26 @@
     out = pl.pallas_call(
         functools.partial(kernel, sections, pair, 32),
         out_shape=jax.ShapeDtypeStruct((width_x, width_y), BF16),
-        in_specs=[anywhere, vmem, vmem, vmem, smem, anywhere, anywhere, vmem],
+        in_specs=[anywhere, vmem, vmem, vmem, smem, anywhere, anywhere, vmem, vmem],
         out_specs=vmem,
         scratch_shapes=[
-            pltpu.VMEM((sections, order, order), slowness.dtype),
+            pltpu.VMEM((sections, order, order), jnp.int16),
+            pltpu.VMEM((width_x, width_y), F32),
+            pltpu.VMEM((width_x, width_y), jnp.int16),
             pltpu.VMEM((slots, 2, order, order), BF16),
             pltpu.VMEM((slots, 2, 2, order, order), BF16),
             pltpu.VMEM((slots, zone_count, 2, order, order), BF16),
-            pltpu.VMEM((sections, 1, 128), jnp.int32),
-            pltpu.SMEM((sections, 1, 128), jnp.int32),
-            pltpu.VMEM((2 * order, 2 * order), BF16),
-            pltpu.VMEM((2 * order, 2 * order), BF16),
+            pltpu.VMEM((8, 128), jnp.int32),
+            pltpu.VMEM((sections, 8, 128), jnp.int32),
+            pltpu.SMEM((sections, 8, 128), jnp.int32),
+            pltpu.VMEM((2, slots, 2, order, order), F32),
+            pltpu.VMEM((slots, 2 * order, 2 * order), BF16),
+            pltpu.VMEM((slots, 2 * order, 2 * order), BF16),
             pltpu.VMEM((sections, order, width_y), BF16),
             pltpu.VMEM((sections, order, width_y), BF16),
             pltpu.VMEM((sections, order, width_y), BF16),
             pltpu.VMEM((order, order), F32),
-            dma((5,)),
+            dma((4,)),
             dma((sections,)), dma((sections,)),
             dma((sections,)), dma((sections,)),
             dma((sections,)), dma((sections,)),
@@ -318,7 +352,7 @@
         compiler_params=pltpu.CompilerParams(collective_id=0, has_side_effects=True),
     )(
         receiver_data, source_amp, source_x.reshape(1, points), source_y.reshape(1, points),
-        omegas, slowness, inverses, zones,
+        omegas, slowness, inverses, zones_x, zones_y,
     )
     return out.astype(F32)[None]
 

time: 29.4 us -> 26.8 us (0.912)
  Pallas kernels: 26.2 us -> 24.8 us
  other arithmetic: 2.52 us -> 1.78 us
  local copies, waits for them, and re-layouts: 0.52 us -> 0 us
    pallas_call x1, Pallas kernels: 26.2 us -> 24.8 us  [per_device(): pl.pallas_call(functools.partial(kernel, sections, pair, 32), out_shape=j...]
    concatenate x1 -> x0, other arithmetic: 0.75 us -> none  [per_device(): zones = jnp.concatenate([zones_x, zones_y], axis=1)]
    pad x1 -> x0, local copies, waits for them, and re-layouts: 0.52 us -> none  [per_device(): zones = jnp.pad(zones, ((0, 0), (0, 128 - zones.shape[1])))]
where the time goes in v2:
time: 26.8 us; the launch traced here: 26.6 us
  Pallas kernels  24.8 us (93%)
  other arithmetic  1.78 us (7%)
    pallas_call x1, Pallas kernels, per_device(): pl.pallas_call(functools.partial(kernel, sections, pair, 32), out_shape=j...  24.8 us
    broadcast_in_dim x1, other arithmetic, per_device(): return out.astype(F32)[None]  1.78 us

profile of v2, /device:TPU:6, one launch (start us, length us, event | category | flops | bytes accessed | tf_op | source)
XLA Modules:
  0.0 26.6 jit_solution(231008598426288084)
XLA Ops:
  0.0 24.8 %shard_map.91 = bf16[1024,128]{1,0:T(8,128)(2,1)} custom-call(bf16[4,2,1024,128]{3,2,1,0:T(8,128)(2,1)} %recv_in.1, bf16[4,2,256]{2,1,0:T(2,128)(2,1)} %amp.1, s32[1,256]{1,0:T(1,128)} %bitcast.5, s32[1,256]{1,0:T(1,128)} %bitcast.6, f32[4]{0:T(128)} %omegas.1, f32[1,1024,128]{2,1,0:T(8,128)} %slow_in.1, bf16[4,4,2,256,256]{4,3,2,1,0:T(8,128)(2,1)} %table_in.1, ...), custom_call_target="tpu_custom_call" | custom-call | tf_op jit(solution)/shard_map/pallas_call | solution.py:322
  24.8 1.8 %bitcast_convert_fusion = f32[1,1024,128]{2,1,0:T(8,128)} fusion(bf16[1024,128]{1,0:T(8,128)(2,1)} %shard_map.91), kind=kLoop, calls=%fused_computation | loop fusion | flops 131072 | bytes 786432 | tf_op jit(solution)/shard_map/broadcast_in_dim | solution.py:357

commit v3 on v2

--- a/solution.py
+++ b/solution.py
@@ -27,8 +27,9 @@
     return [float(term) for term in fit.convert(kind=np.polynomial.Polynomial).coef]
 
 
-SIN_TERMS = fitted(lambda t: np.sin(t) / t, 6)
-COS_TERMS = fitted(np.cos, 6)
+ROOT2 = math.sqrt(2.0)
+SIN_TERMS = fitted(lambda t: ROOT2 * np.sin(t) / t, 5)
+COS_TERMS = fitted(lambda t: -ROOT2 * np.cos(t), 5)
 
 
 def series(square, terms):
@@ -40,10 +41,8 @@
 
 def sincos(half):
     square = half * half
-    sine = series(square, SIN_TERMS) * half
-    cosine = series(square, COS_TERMS)
-    double = sine + sine
-    return -(double * cosine), double * sine - 1.0
+    root_sine = series(square, SIN_TERMS) * half
+    return root_sine * series(square, COS_TERMS), root_sine * root_sine - 1.0
 
 
 def block_form(blocks):
@@ -129,6 +128,34 @@
     )
     rec_copy.start()
 
+    def arrived_slow(level):
+        return pltpu.make_async_remote_copy(
+            src_ref=slow.at[level, :, mine], dst_ref=slow.at[level, :, mine],
+            send_sem=slow_send.at[0], recv_sem=slow_recv.at[level],
+            device_id=(d, mate_line), device_id_type=MESH,
+        )
+
+    def forward(level, half):
+        return pltpu.make_async_remote_copy(
+            src_ref=slow.at[level, :, half], dst_ref=slow.at[level, :, half],
+            send_sem=fwd_send.at[level], recv_sem=fwd_recv.at[level],
+            device_id=(d, mate_line), device_id_type=MESH,
+        )
+
+    def turn(level, lanes):
+        for slot in range(slots):
+            omega = omegas[q * slots + slot]
+            slope = omega * (0.5 * CODE_STEP)
+            shift = omega * (0.5 * SLOW_MID) - 0.5 * math.pi
+            for start in range(0, order, rows):
+                part = slice(start, start + rows)
+                value = slow[level, part, lanes].astype(jnp.int32).astype(F32)
+                sine, cosine = sincos(value * slope + shift)
+                trig[level, slot, 0, part, lanes] = sine
+                trig[level, slot, 1, part, lanes] = cosine
+
+    forward(d, mine).start()
+
     points = src_x.shape[1]
     cells = lax.broadcasted_iota(jnp.int32, (order, points), 0)
     hit_x = cells + d * order == src_x[...]
@@ -142,35 +169,14 @@
             )
             wave[slot, 0, part] = field.astype(BF16)
 
-    def arrived_slow(level):
-        return pltpu.make_async_remote_copy(
-            src_ref=slow.at[level, :, mine], dst_ref=slow.at[level, :, mine],
-            send_sem=slow_send.at[0], recv_sem=slow_recv.at[level],
-            device_id=(d, mate_line), device_id_type=MESH,
-        )
-
-    def forward(level, half):
-        return pltpu.make_async_remote_copy(
-            src_ref=slow.at[level, :, half], dst_ref=slow.at[level, :, half],
-            send_sem=fwd_send.at[level], recv_sem=fwd_recv.at[level],
-            device_id=(d, mate_line), device_id_type=MESH,
-        )
-
-    def relay(level):
-        @pl.when(level != d)
-        def _():
-            arrived_slow(level).wait_recv()
-
-        forward(level, mine).start()
-
-    relay(0)
-
     local[1].wait()
     rec_copy.wait_recv()
     for slot in range(slots):
         wave[slot, 1, 0] = rec[slot, 0]
         wave[slot, 1, 1] = -rec[slot, 1]
     local[2].wait()
+    forward(d, theirs).wait_recv()
+    turn(d, slice(0, order))
     for level in range(sections):
         @pl.when(level != d)
         def _():
@@ -181,23 +187,19 @@
     zone_copy = pltpu.make_async_copy(zone_buf, zone_rows, local_sems.at[3])
     zone_copy.start()
     zone_copy.wait()
-    forward(0, theirs).wait_recv()
-
-    def turn(level, slot):
-        omega = omegas[q * slots + slot]
-        slope = omega * (0.5 * CODE_STEP)
-        shift = omega * (0.5 * SLOW_MID) - 0.5 * math.pi
-        for start in range(0, order, rows):
-            part = slice(start, start + rows)
-            value = slow[level, part, :].astype(jnp.int32).astype(F32)
-            sine, cosine = sincos(value * slope + shift)
-            trig[level % 2, slot, 0, part, :] = sine
-            trig[level % 2, slot, 1, part, :] = cosine
+
+    @pl.when(d != 0)
+    def _():
+        arrived_slow(0).wait_recv()
+        forward(0, mine).start()
+        turn(0, mine)
+        forward(0, theirs).wait_recv()
+        turn(0, theirs)
 
     def rotate(level, slot):
         for start in range(0, order, rows):
             part = slice(start, start + rows)
-            sine, cosine = trig[level % 2, slot, 0, part, :], trig[level % 2, slot, 1, part, :]
+            sine, cosine = trig[level, slot, 0, part, :], trig[level, slot, 1, part, :]
             for field in range(2):
                 real = wave[slot, field, 0, part, :].astype(F32)
                 imag = wave[slot, field, 1, part, :].astype(F32)
@@ -227,10 +229,10 @@
             solved = value[:, lanes].astype(F32) + lax.dot_general(
                 value, m_y[lanes], (((1,), (1,)), ((), ())), preferred_element_type=F32
             )
-            solved = solved.astype(BF16)
-            wave[slot, 0, part] = solved[:order]
-            wave[slot, 1, part] = solved[order:]
-            product.append(solved[:order].astype(F32) * solved[order:].astype(F32))
+            product.append(solved[:order] * solved[order:])
+            if level + 1 < sections:
+                wave[slot, 0, part] = solved[:order].astype(BF16)
+                wave[slot, 1, part] = solved[order:].astype(BF16)
         image = (omega * omega) * (product[0] - product[1])
         if slot == 0:
             total[...] = image
@@ -265,26 +267,26 @@
             deliver_copy(level).start()
 
     for level in range(sections):
+        if level > 0:
+            @pl.when(level != d)
+            def _():
+                forward(level, theirs).wait_recv()
+                turn(level, slice(0, order))
+
         if level + 1 < sections:
-            relay(level + 1)
-            if level > 0:
-                forward(level + 1, theirs).wait_recv()
+            @pl.when(level + 1 != d)
+            def _():
+                arrived_slow(level + 1).wait_recv()
+                forward(level + 1, mine).start()
+
         if level > 0:
             deliver(level - 1)
-        if level < 2:
-            for slot in range(slots):
-                turn(level, slot)
         for stage in (rotate, solve_inline, solve_crossline):
             for slot in range(slots):
                 stage(level, slot)
-        if 0 < level < sections - 1:
-            for slot in range(slots):
-                turn(level + 1, slot)
         own[level] = total[:, mine].astype(BF16)
         sent[level] = total[:, theirs].astype(BF16)
         swap(level).start()
-        if level == 0:
-            forward(1, theirs).wait_recv()
     deliver(sections - 1)
 
     for copy in zone_copies + slow_copies:
@@ -321,7 +323,7 @@
     dma = pltpu.SemaphoreType.DMA
     out = pl.pallas_call(
         functools.partial(kernel, sections, pair, 32),
-        out_shape=jax.ShapeDtypeStruct((width_x, width_y), BF16),
+        out_shape=pltpu.VMEM((width_x, width_y), BF16),
         in_specs=[anywhere, vmem, vmem, vmem, smem, anywhere, anywhere, vmem, vmem],
         out_specs=vmem,
         scratch_shapes=[
@@ -334,7 +336,7 @@
             pltpu.VMEM((8, 128), jnp.int32),
             pltpu.VMEM((sections, 8, 128), jnp.int32),
             pltpu.SMEM((sections, 8, 128), jnp.int32),
-            pltpu.VMEM((2, slots, 2, order, order), F32),
+            pltpu.VMEM((sections, slots, 2, order, order), F32),
             pltpu.VMEM((slots, 2 * order, 2 * order), BF16),
             pltpu.VMEM((slots, 2 * order, 2 * order), BF16),
             pltpu.VMEM((sections, order, width_y), BF16),

time: 26.8 us -> 22.9 us (0.85)
  Pallas kernels: 24.8 us -> 21.7 us
  other arithmetic: 1.78 us -> 0.83 us
    pallas_call x1, Pallas kernels: 24.8 us -> 21.7 us  [per_device(): pl.pallas_call(functools.partial(kernel, sections, pair, 32), out_shape=p...]
    broadcast_in_dim x1, other arithmetic: 1.78 us -> 0.83 us  [per_device(): return out.astype(F32)[None]]
where the time goes in v3:
time: 22.9 us; the launch traced here: 22.5 us
  Pallas kernels  21.7 us (95%)
  other arithmetic  0.83 us (4%)
    pallas_call x1, Pallas kernels, per_device(): pl.pallas_call(functools.partial(kernel, sections, pair, 32), out_shape=p...  21.7 us
    broadcast_in_dim x1, other arithmetic, per_device(): return out.astype(F32)[None]  0.83 us

profile of v3, /device:TPU:6, one launch (start us, length us, event | category | flops | bytes accessed | tf_op | source)
XLA Modules:
  0.0 22.5 jit_solution(7682069045666603640)
XLA Ops:
  0.0 21.7 %shard_map.91 = bf16[1024,128]{1,0:T(8,128)(2,1)S(1)} custom-call(bf16[4,2,1024,128]{3,2,1,0:T(8,128)(2,1)} %recv_in.1, bf16[4,2,256]{2,1,0:T(2,128)(2,1)} %amp.1, s32[1,256]{1,0:T(1,128)} %bitcast.5, s32[1,256]{1,0:T(1,128)} %bitcast.6, f32[4]{0:T(128)} %omegas.1, f32[1,1024,128]{2,1,0:T(8,128)} %slow_in.1, bf16[4,4,2,256,256]{4,3,2,1,0:T(8,128)(2,1)} %table_in.1, ...), custom_call_target="tpu_custom_call" | custom-call | tf_op jit(solution)/shard_map/pallas_call | solution.py:324
  21.7 0.8 %bitcast_convert_fusion = f32[1,1024,128]{2,1,0:T(8,128)} fusion(bf16[1024,128]{1,0:T(8,128)(2,1)S(1)} %shard_map.91), kind=kLoop, calls=%fused_computation | loop fusion | flops 131072 | bytes 786432 | tf_op jit(solution)/shard_map/broadcast_in_dim | solution.py:359

commit v4 on v3

--- a/solution.py
+++ b/solution.py
@@ -50,6 +50,13 @@
     top = jnp.concatenate([k_real, -k_imag], axis=1)
     bottom = jnp.concatenate([k_imag, k_real], axis=1)
     return jnp.concatenate([top, bottom], axis=0)
+
+
+def flip(index, bits):
+    for bit in (1, 2, 4, 8):
+        if bits & bit:
+            index = index + bit - 2 * bit * lax.rem(index // bit, 2)
+    return index
 
 
 def kernel(
@@ -76,7 +83,7 @@
 
     barrier = pltpu.get_barrier_semaphore()
     pl.semaphore_signal(barrier, inc=1, device_id=(d, mate_line), device_id_type=MESH)
-    others = [lax.rem(d + k, sections) for k in range(1, sections)]
+    others = [flip(d, k) for k in range(1, sections)]
     for other in others:
         pl.semaphore_signal(barrier, inc=1, device_id=(other, line), device_id_type=MESH)
 
@@ -188,26 +195,37 @@
     zone_copy.start()
     zone_copy.wait()
 
+    def rotate(level, slot, base=0, size=order):
+        near = pl.ds(base, size) if size == order else pl.ds(pl.multiple_of(base, size), size)
+        for start in range(0, order, rows):
+            part = slice(start, start + rows)
+            sine, cosine = trig[level, slot, 0, part, near], trig[level, slot, 1, part, near]
+            for field in range(2):
+                real = wave[slot, field, 0, part, near].astype(F32)
+                imag = wave[slot, field, 1, part, near].astype(F32)
+                if size == order:
+                    lanes = pl.ds(field * order, order)
+                else:
+                    lanes = pl.ds(pl.multiple_of(field * order + base, size), size)
+                rotated[slot, part, lanes] = (real * cosine - imag * sine).astype(BF16)
+                rotated[slot, order + start:order + start + rows, lanes] = (
+                    real * sine + imag * cosine
+                ).astype(BF16)
+
+    @pl.when(d == 0)
+    def _():
+        for slot in range(slots):
+            rotate(0, slot, q * width, width)
+
     @pl.when(d != 0)
     def _():
         arrived_slow(0).wait_recv()
         forward(0, mine).start()
         turn(0, mine)
+        for slot in range(slots):
+            rotate(0, slot, q * width, width)
         forward(0, theirs).wait_recv()
         turn(0, theirs)
-
-    def rotate(level, slot):
-        for start in range(0, order, rows):
-            part = slice(start, start + rows)
-            sine, cosine = trig[level, slot, 0, part, :], trig[level, slot, 1, part, :]
-            for field in range(2):
-                real = wave[slot, field, 0, part, :].astype(F32)
-                imag = wave[slot, field, 1, part, :].astype(F32)
-                lanes = slice(field * order, (field + 1) * order)
-                rotated[slot, part, lanes] = (real * cosine - imag * sine).astype(BF16)
-                rotated[slot, order + start:order + start + rows, lanes] = (
-                    real * sine + imag * cosine
-                ).astype(BF16)
 
     def solve_inline(level, slot):
         m_x = block_form(table[slot, zone_rows[level, 0, d]])
@@ -281,7 +299,12 @@
 
         if level > 0:
             deliver(level - 1)
-        for stage in (rotate, solve_inline, solve_crossline):
+        for slot in range(slots):
+            if level == 0:
+                rotate(0, slot, (1 - q) * width, width)
+            else:
+                rotate(level, slot)
+        for stage in (solve_inline, solve_crossline):
             for slot in range(slots):
                 stage(level, slot)
         own[level] = total[:, mine].astype(BF16)
@@ -317,6 +340,7 @@
     zone_count = inverses.shape[1]
     slots = freqs // pair
     assert pair == 2 and width_x == order * sections and slowness.shape[0] == 1
+    assert sections & (sections - 1) == 0
     vmem = pl.BlockSpec(memory_space=pltpu.VMEM)
     smem = pl.BlockSpec(memory_space=pltpu.SMEM)
     anywhere = pl.BlockSpec(memory_space=pl.ANY)

time: 22.9 us -> 23.1 us (level)
  no operation moved by 1% of the time
where the time goes in v4:
time: 23.1 us; the launch traced here: 22.7 us
  Pallas kernels  21.8 us (94%)
  other arithmetic  0.83 us (4%)
    pallas_call x1, Pallas kernels, per_device(): pl.pallas_call(functools.partial(kernel, sections, pair, 32), out_shape=p...  21.8 us
    broadcast_in_dim x1, other arithmetic, per_device(): return out.astype(F32)[None]  0.83 us

profile of v4, /device:TPU:6, one launch (start us, length us, event | category | flops | bytes accessed | tf_op | source)
XLA Modules:
  0.0 22.7 jit_solution(6169652353075369827)
XLA Ops:
  0.0 21.8 %shard_map.91 = bf16[1024,128]{1,0:T(8,128)(2,1)S(1)} custom-call(bf16[4,2,1024,128]{3,2,1,0:T(8,128)(2,1)} %recv_in.1, bf16[4,2,256]{2,1,0:T(2,128)(2,1)} %amp.1, s32[1,256]{1,0:T(1,128)} %bitcast.5, s32[1,256]{1,0:T(1,128)} %bitcast.6, f32[4]{0:T(128)} %omegas.1, f32[1,1024,128]{2,1,0:T(8,128)} %slow_in.1, bf16[4,4,2,256,256]{4,3,2,1,0:T(8,128)(2,1)} %table_in.1, ...), custom_call_target="tpu_custom_call" | custom-call | tf_op jit(solution)/shard_map/pallas_call | solution.py:348
  21.8 0.8 %bitcast_convert_fusion = f32[1,1024,128]{2,1,0:T(8,128)} fusion(bf16[1024,128]{1,0:T(8,128)(2,1)S(1)} %shard_map.91), kind=kLoop, calls=%fused_computation | loop fusion | flops 131072 | bytes 786432 | tf_op jit(solution)/shard_map/broadcast_in_dim | solution.py:383
